TPU v7x, 32 devices: a whole 2x2x4 slice. The times are simulated.
32 devices in a mesh: grp: 2 (over y), patch: 8 (over z, x), frame: 2 (over core).
Axes of the slice: x: 2, y: 2, z: 4, core: 2. Of those that a mesh axis runs over, the one named last changes fastest.
Arguments:
- video_tokens: bfloat16 [4, 16, 80, 1152], P('grp', 'frame', 'patch'), parts along dimension 0, may hold values from -6 to 6
- timestep: int32 [2], P('grp'), parts along dimension 0, may hold values from 0 to 999
- w_qkv: bfloat16 [2, 1152, 1728], P(None, 'patch'), may hold values from -0.1875 to 0.1875
- w_out: bfloat16 [2, 576, 1152], P(None, None, 'patch'), may hold values from -0.25 to 0.25
- qk_gain: float32 [2, 2, 72], replicated, may hold values from 1 to 2.5
- mod_table: float32 [2, 3, 1152], replicated, may hold values from -3 to 3
- mod_gain: float32 [2, 3, 1152], replicated, may hold values from -3 to 3
Outputs:
- denoised: bfloat16 [4, 16, 80, 1152], P('grp', 'frame', 'patch'), parts along dimension 0
There are 2 independent parts, one for each index of `grp`. A program takes and returns all parts, laid end to end along the dimension named above; an argument that names none is the same for every part. Nothing has to cross between parts.
All inputs are finite; a program needn't handle non-finite values.
Results may differ from a plain program's by a relative error of at most 0.013.
Values may be sent and summed in bfloat16 or wider, within the bound.
A program may use at most 128 MiB of HBM per device.

v0:
```python
import math
import jax
import jax.numpy as jnp
from jax import lax
from jax.sharding import PartitionSpec as P


def time_embed(timestep, width):
    half_width = width // 2
    freqs = jnp.exp(-math.log(10000.0) * jnp.arange(half_width, dtype=jnp.float32) / half_width)
    angles = timestep[0].astype(jnp.float32) * freqs
    return jnp.concatenate([jnp.cos(angles), jnp.sin(angles)])


def modulate(tokens, table, gains, embed):
    params = table + gains * embed[None, :]
    values = tokens.astype(jnp.float32)
    centre = jnp.mean(values, axis=-1, keepdims=True)
    centred = values - centre
    spread = jnp.mean(centred * centred, axis=-1, keepdims=True)
    normed = centred * lax.rsqrt(spread + 1e-06)
    return ((normed * (1.0 + params[1]) + params[0]).astype(jnp.bfloat16), params[2])


def head_norm(values, gain):
    meansq = jnp.mean(values * values, axis=-1, keepdims=True)
    return (values * lax.rsqrt(meansq + 1e-06) * gain).astype(jnp.bfloat16)


def fetch_weights(qkv_rows, out_cols):
    return (
        lax.all_gather(qkv_rows, "patch", axis=0, tiled=True),
        lax.all_gather(out_cols, "patch", axis=1, tiled=True),
    )


def attend_items(stacked):
    head_size = stacked.shape[-1]
    query = stacked[0, 0]
    key = stacked[1, 0]
    value = stacked[2, 0]
    scores = jnp.einsum("nqd,nkd->nqk", query, key, preferred_element_type=jnp.float32) / math.sqrt(
        head_size
    )
    raised = jnp.exp(scores)
    total = jnp.sum(raised, axis=-1, keepdims=True)
    summed = jnp.einsum(
        "nqk,nkd->nqd", raised.astype(jnp.bfloat16), value, preferred_element_type=jnp.float32
    )
    return (summed / total).astype(jnp.bfloat16)[None]


def spatial(query, key, value, videos, fr_dev, patch_dev):
    rows, heads, head_size = query.shape
    groups = lax.axis_size("patch")
    per_group = videos * fr_dev * heads // groups
    stacked = jnp.stack([query, key, value])
    stacked = stacked.reshape(3, videos * fr_dev, patch_dev, heads, head_size)
    stacked = stacked.transpose(0, 1, 3, 2, 4).reshape(3, groups, per_group, patch_dev, head_size)
    attended = attend_items(
        lax.all_to_all(stacked, "patch", split_axis=1, concat_axis=3, tiled=True)
    )
    returned = lax.all_to_all(attended, "patch", split_axis=2, concat_axis=0, tiled=True)
    returned = returned.reshape(videos * fr_dev, heads, patch_dev, head_size).transpose(0, 2, 1, 3)
    return returned.reshape(rows, heads * head_size)


def frame_attend(query, key, value, heads):
    videos, q_frames, patches, feat = query.shape
    k_frames = key.shape[1]
    head_size = feat // heads
    query = query.reshape(videos, q_frames, patches, heads, head_size)
    key = key.reshape(videos, k_frames, patches, heads, head_size)
    value = value.reshape(videos, k_frames, patches, heads, head_size)
    scores = jnp.einsum(
        "bfphd,bgphd->bphfg", query, key, preferred_element_type=jnp.float32
    ) / math.sqrt(head_size)
    raised = jnp.exp(scores)
    total = jnp.sum(raised, axis=-1)
    summed = jnp.einsum(
        "bphfg,bgphd->bfphd", raised.astype(jnp.bfloat16), value, preferred_element_type=jnp.float32
    )
    result = summed / total.transpose(0, 3, 1, 2)[..., None]
    return result.astype(jnp.bfloat16).reshape(videos, q_frames, patches, feat)


def temporal(query, key, value, videos, fr_dev, patch_dev):
    rows, heads, head_size = query.shape
    feat = heads * head_size
    query4 = query.reshape(videos, fr_dev, patch_dev, feat)
    key4 = key.reshape(videos, fr_dev, patch_dev, feat)
    value4 = value.reshape(videos, fr_dev, patch_dev, feat)
    joined = jnp.concatenate([query4, key4, value4], axis=3)
    swapped = lax.all_to_all(joined, "frame", split_axis=2, concat_axis=1, tiled=True)
    result = frame_attend(
        swapped[..., :feat], swapped[..., feat : 2 * feat], swapped[..., 2 * feat :], heads
    )
    returned = lax.all_to_all(result, "frame", split_axis=1, concat_axis=2, tiled=True)
    return returned.reshape(rows, feat)


def per_device(video_tokens, timestep, w_qkv, w_out, qk_gain, mod_table, mod_gain):
    videos, fr_dev, patch_dev, width = video_tokens.shape
    rows = videos * fr_dev * patch_dev
    head_size = qk_gain.shape[2]
    heads = w_out.shape[1] // head_size
    embed = time_embed(timestep, width)
    tokens = video_tokens.reshape(rows, width)
    for layer in range(2):
        qkv_full, out_full = fetch_weights(w_qkv[layer], w_out[layer])
        mixed, gate = modulate(tokens, mod_table[layer], mod_gain[layer], embed)
        joint = jnp.dot(mixed, qkv_full, preferred_element_type=jnp.float32)
        joint = joint.reshape(rows, 3, heads, head_size)
        query = head_norm(joint[:, 0], qk_gain[layer, 0])
        key = head_norm(joint[:, 1], qk_gain[layer, 1])
        value = joint[:, 2].astype(jnp.bfloat16)
        if layer == 0:
            attended = spatial(query, key, value, videos, fr_dev, patch_dev)
        else:
            attended = temporal(query, key, value, videos, fr_dev, patch_dev)
        update = jnp.dot(attended, out_full, preferred_element_type=jnp.float32)
        tokens = (tokens.astype(jnp.float32) + gate * update).astype(jnp.bfloat16)
    return tokens.reshape(videos, fr_dev, patch_dev, width)


def solution(mesh):
    placed = (
        P("grp", "frame", "patch", None),
        P("grp"),
        P(None, "patch", None),
        P(None, None, "patch"),
        P(),
        P(),
        P(),
    )
    return jax.shard_map(
        per_device,
        mesh=mesh,
        in_specs=placed,
        out_specs=P("grp", "frame", "patch", None),
        check_vma=False,
    )
```

profile of v0, /device:TPU:0, one launch (start us, length us, event | category | flops | bytes accessed | tf_op | source)
XLA Modules:
  0.0 268.2 jit_solution(7167278873392558477)
XLA Ops:
  6.6 2.3 fusion.36
  9.0 0.8 fusion.39
  9.8 0.7 all-gather.13.cloned.1.call-update
  11.6 0.2 multiply_reduce_fusion.1
  11.8 0.3 add_convert_fusion.1
  12.4 72.5 %all-gather.9.cloned.1.call-done = bf16[1,1152,1728]{2,1,0:T(8,128)(2,1)} async-done(((bf16[1,144,1728]{2,1,0:T(8,128)(2,1)}), bf16[1,1152,1728]{2,1,0:T(8,128)(2,1)}) %all-gather.9.cloned.1.call-update) | async-done | bytes 3981328 | tf_op jit(solution)/shard_map/all_gather | solution.py:32
  84.8 6.5 %copy.88 = bf16[1728,1152]{1,0:T(8,128)(2,1)} copy(bf16[1728,1152]{0,1:T(8,128)(2,1)} %bitcast.115) | data formatting | bytes 7962624 | tf_op jit(solution)/shard_map/dot_general | solution.py:112
  91.4 3.6 %fusion.15 = f32[160,3,8,72]{0,3,2,1:T(8,128)S(1)} fusion(bf16[3,8,72,1152]{3,2,1,0:T(8,128)(2,1)} %bitcast.116, bf16[160,1152,1,1]{1,0,2,3:T(8,128)(2,1)S(1)} %reshape.231), kind=kOutput, calls=%fused_computation.38 | convolution fusion | flops 637009920 | bytes 5455872 | tf_op jit(solution)/shard_map/dot_general | solution.py:112
  95.2 0.3 copy.89
  95.8 0.3 copy.91
  96.4 0.2 copy.93
  96.6 0.2 multiply_convert_fusion.3
  96.9 0.2 multiply_convert_fusion.2
  97.1 0.2 maximum_bitcast_fusion
  97.4 0.3 copy.94
  97.8 40.4 %all_to_all.63 = bf16[3,8,16,10,72]{4,2,3,0,1:T(8,128)(2,1)S(1)} all-to-all(bf16[3,8,16,10,72]{4,2,3,0,1:T(8,128)(2,1)S(1)} %copy.95), channel_id=1, replica_groups=mesh['grp'=2,'patch'=8,'frame'=2] {'patch'}, dimensions={1} | all-to-all | bytes 1105920 | tf_op jit(solution)/shard_map/all_to_all | solution.py:61
  138.3 0.3 fusion.42
  138.7 0.4 fusion.14
  139.1 1.0 copy.100
  140.1 3.7 %all-to-all-start.1 = ((bf16[1,16,80,72]{3,1,0,2:T(8,128)(2,1)}), bf16[1,16,80,72]{3,1,0,2:T(8,128)(2,1)S(1)}, u32[]{:S(2)}, u32[]{:S(2)}) async-start(bf16[1,16,80,72]{3,1,0,2:T(8,128)(2,1)} %copy.100), calls=%async_computation.1 | async-start | bytes 655360 | tf_op jit(solution)/shard_map/all_to_all | solution.py:63
  144.0 0.3 all-gather.15.cloned.1.call-update
  144.7 15.2 %all-to-all-done.1 = bf16[1,16,80,72]{3,1,0,2:T(8,128)(2,1)S(1)} async-done(((bf16[1,16,80,72]{3,1,0,2:T(8,128)(2,1)}), bf16[1,16,80,72]{3,1,0,2:T(8,128)(2,1)S(1)}, u32[]{:S(2)}, u32[]{:S(2)}) %all-to-all-start.1) | async-done | bytes 184352 | tf_op jit(solution)/shard_map/all_to_all | solution.py:63
  160.3 2.1 fusion.43
  162.6 52.2 %all-gather.13.cloned.1.call-done = bf16[1,1152,1728]{2,1,0:T(8,128)(2,1)} async-done(((bf16[1,144,1728]{2,1,0:T(8,128)(2,1)}), bf16[1,1152,1728]{2,1,0:T(8,128)(2,1)}) %all-gather.13.cloned.1.call-update) | async-done | bytes 3981328 | tf_op jit(solution)/shard_map/all_gather | solution.py:32
  214.8 4.2 %fusion = f32[160,1728]{1,0:T(8,128)} fusion(bf16[1,1152,1728]{2,1,0:T(8,128)(2,1)} %all-gather.13.cloned.1.call-done, f32[160,1152]{1,0:T(8,128)S(1)} %get-tuple-element.42, f32[1152]{0:T(1024)S(1)} %get-tuple-element.10, f32[1152]{0:T(1024)S(1)} %get-tuple-element.11, f32[160]{0:T(256)S(1)} %add_rsqrt_fusion.5, f32[160]{0:T(256)S(1)} %broadcast_multiply_fusion.1), kind=kOutput, calls=%fused_computation | convolution fusion | flops 637931520 | bytes 5835008 | tf_op jit(solution)/shard_map/dot_general | solution.py:112
  219.0 2.2 reshape.219
  221.2 0.8 slice.163
  222.0 1.1 multiply_reduce_fusion.2
  223.5 0.3 mul.268
  223.8 0.3 squeeze.63
  224.3 0.2 mul.258
  224.6 0.3 mul.259
  224.9 1.4 squeeze.62
  226.2 2.1 convert_element_type.113
  228.3 0.8 multiply_convert_fusion
  229.1 0.8 multiply_convert_fusion.1
  230.1 1.4 concatenate.8
  231.6 4.2 %all_to_all.64 = bf16[2,8,10,1728]{3,1,0,2:T(8,128)(2,1)S(1)} all-to-all(bf16[2,8,10,1728]{3,1,0,2:T(8,128)(2,1)S(1)} %copy.108), channel_id=1, replica_groups=mesh['grp'=2,'patch'=8,'frame'=2] {'frame'}, dimensions={2} | all-to-all | bytes 1105920 | tf_op jit(solution)/shard_map/all_to_all | solution.py:94
  236.0 0.3 reshape.221
  236.3 0.3 reshape.222
  236.7 0.3 reshape.220
  237.0 0.4 fusion.44
  237.4 0.4 fusion.12
  237.9 0.6 reshape.233
  238.5 3.9 %all_to_all.65 = bf16[2,16,5,576]{3,0,2,1:T(2,128)(2,1)S(1)} all-to-all(bf16[2,16,5,576]{3,0,2,1:T(2,128)(2,1)S(1)} %reshape.233), channel_id=1, replica_groups=mesh['grp'=2,'patch'=8,'frame'=2] {'frame'}, dimensions={1} | all-to-all | bytes 368640 | tf_op jit(solution)/shard_map/all_to_all | solution.py:98
  242.5 16.2 %all-gather.15.cloned.1.call-done = bf16[1,576,1152]{1,2,0:T(8,128)(2,1)} async-done(((bf16[1,576,144]{1,2,0:T(8,128)(2,1)}), bf16[1,576,1152]{1,2,0:T(8,128)(2,1)}) %all-gather.15.cloned.1.call-update) | async-done | bytes 1327120 | tf_op jit(solution)/shard_map/all_gather | solution.py:33
  258.8 2.0 fusion.6
  260.9 0.8 copy.118
  (67 shorter events, 4.5 us)
Async XLA Ops:
  6.5 2.4 copy-start.2
  6.5 4.8 %copy-start.4 = (f32[2,3,1152]{2,0,1:T(2,128)S(1)}, f32[2,3,1152]{2,0,1:T(2,128)}, u32[]{:S(2)}) copy-start(f32[2,3,1152]{2,0,1:T(2,128)} %param.12) | copy-start | bytes 82948
  6.5 4.8 %copy-start.3 = (f32[2,3,1152]{2,0,1:T(2,128)S(1)}, f32[2,3,1152]{2,0,1:T(2,128)}, u32[]{:S(2)}) copy-start(f32[2,3,1152]{2,0,1:T(2,128)} %param.13) | copy-start | bytes 82948
  6.5 4.9 %copy-start = (bf16[2,8,10,1152]{3,1,2,0:T(8,128)(2,1)S(1)}, bf16[2,8,10,1152]{3,1,2,0:T(8,128)(2,1)}, u32[]{:S(2)}) copy-start(bf16[2,8,10,1152]{3,1,2,0:T(8,128)(2,1)} %param.7) | copy-start | bytes 1105924
  6.5 78.3 %all-gather.9.cloned.1.call-start = ((), (), s32[]{:S(2)}) async-start(), calls=%async_computation.4 | async-start | bytes 4644864 | tf_op jit(solution)/shard_map/all_gather | solution.py:32
  8.9 151.4 %all-gather.11.cloned.1.call-start = ((), (), s32[]{:S(2)}) async-start(), calls=%async_computation.5 | async-start | bytes 1658880 | tf_op jit(solution)/shard_map/all_gather | solution.py:33
  9.8 205.1 %all-gather.13.cloned.1.call-start = ((), (), s32[]{:S(2)}) async-start(), calls=%async_computation.6 | async-start | bytes 4644864 | tf_op jit(solution)/shard_map/all_gather | solution.py:32
  11.4 0.9 copy-start.5
  140.1 19.9 %all-to-all-start.1 = ((bf16[1,16,80,72]{3,1,0,2:T(8,128)(2,1)}), bf16[1,16,80,72]{3,1,0,2:T(8,128)(2,1)S(1)}, u32[]{:S(2)}, u32[]{:S(2)}) async-start(bf16[1,16,80,72]{3,1,0,2:T(8,128)(2,1)} %copy.100), calls=%async_computation.1 | async-start | bytes 655360 | tf_op jit(solution)/shard_map/all_to_all | solution.py:63
  143.7 115.0 %all-gather.15.cloned.1.call-start = ((), (), s32[]{:S(2)}) async-start(), calls=%async_computation.7 | async-start | bytes 1658880 | tf_op jit(solution)/shard_map/all_gather | solution.py:33
  229.1 1.0 copy-start.1
Sparse Core Ops, SparseCore 0:
  9.6 75.2 all-gather.8
  87.0 51.2 all-gather.10
  140.5 74.2 all-gather.12
  216.9 41.8 all-gather.14
where the time goes:
time: 269 us; the launch traced here: 268 us
  waiting for transfers between devices  157 us (58%)
  blocking collectives  48.4 us (18%)
  local copies, waits for them, and re-layouts  26.3 us (10%)
  between operations  14.2 us (5%)
  matrix products  13.3 us (5%)
  other arithmetic  4.76 us (2%)
  starting transfers between devices  4 us (1%)
    all_gather x2, waiting for transfers between devices, fetch_weights(): lax.all_gather(qkv_rows, 'patch', axis=0, tiled=True)  125 us
    all_to_all x1, blocking collectives, spatial(): lax.all_to_all(stacked, 'patch', split_axis=1, concat_axis=3, tiled=True)  40.4 us
    all_gather x2, waiting for transfers between devices, fetch_weights(): lax.all_gather(out_cols, 'patch', axis=1, tiled=True)  16.3 us
    all_to_all x1, waiting for transfers between devices, spatial(): lax.all_to_all(attended, 'patch', split_axis=2, concat_axis=0, tiled=True)  15.2 us
    dot_general x2, matrix products, per_device(): joint = jnp.dot(mixed, qkv_full, preferred_element_type=jnp.float32)  7.8 us
    dot_general x1, local copies, waits for them, and re-layouts, per_device(): joint = jnp.dot(mixed, qkv_full, preferred_element_type=jnp.float32)  6.5 us
  transfers between devices with their start and end apart: 5, of which 4 were waited for; matrix products, arithmetic and copies ran while one was open for 15% of the time, Pallas kernels for 0%

commit v1 on v0

--- a/solution.py
+++ b/solution.py
@@ -3,6 +3,16 @@
 import jax.numpy as jnp
 from jax import lax
 from jax.sharding import PartitionSpec as P
+
+
+def ring_gather(x, axis, dim):
+    ways, here, step = (lax.axis_size(axis), lax.axis_index(axis), x.shape[dim])
+    shape = [n * ways if d == dim else n for d, n in enumerate(x.shape)]
+    full = lax.dynamic_update_slice_in_dim(jnp.zeros(shape, x.dtype), x, here * step, axis=dim)
+    for far in range(1, ways):
+        x = lax.ppermute(x, axis, [(d, (d + 1) % ways) for d in range(ways)])
+        full = lax.dynamic_update_slice_in_dim(full, x, (here - far) % ways * step, axis=dim)
+    return full
 
 
 def time_embed(timestep, width):
@@ -30,7 +40,7 @@
 def fetch_weights(qkv_rows, out_cols):
     return (
         lax.all_gather(qkv_rows, "patch", axis=0, tiled=True),
-        lax.all_gather(out_cols, "patch", axis=1, tiled=True),
+        ring_gather(out_cols, "patch", 1),
     )
 
 

time: 269 us -> 264 us (0.981)
  blocking collectives: 48.4 us -> 8.05 us
  starting transfers between devices: 4 us -> 31.1 us
  local copies, waits for them, and re-layouts: 26.3 us -> 44.8 us
  waiting for transfers between devices: 157 us -> 146 us
  other arithmetic: 4.76 us -> 7.68 us
  matrix products: 13.3 us -> 10.6 us
    ppermute x0 -> x14, waiting for transfers between devices: none -> 72.6 us  [ring_gather(): x = lax.ppermute(x, axis, [(d, (d + 1) % ways) for d in range(ways)])]
    all_gather x2, waiting for transfers between devices: 125 us -> 66.3 us  [fetch_weights(): lax.all_gather(qkv_rows, 'patch', axis=0, tiled=True)]
    all_to_all x1 -> x0, blocking collectives: 40.4 us -> none  [spatial(): lax.all_to_all(stacked, 'patch', split_axis=1, concat_axis=3, tiled=True)]
    ppermute x0 -> x14, starting transfers between devices: none -> 22.8 us  [ring_gather(): x = lax.ppermute(x, axis, [(d, (d + 1) % ways) for d in range(ways)])]
    all_gather x2 -> x0, waiting for transfers between devices: 16.3 us -> none  [fetch_weights(): lax.all_gather(out_cols, 'patch', axis=1, tiled=True)]
    dynamic_update_slice x0 -> x15, local copies, waits for them, and re-layouts: none -> 9.74 us  [the longest x13 9.68 us: ring_gather(): lax.dynamic_update_slice_in_dim(full, x, (here - far) % ways * step, axis...]
    all_to_all x1, waiting for transfers between devices: 15.2 us -> 7.27 us  [spatial(): lax.all_to_all(attended, 'patch', split_axis=2, concat_axis=0, tiled=True)]
    all_to_all x0 -> x1, starting transfers between devices: none -> 3.55 us  [spatial(): lax.all_to_all(stacked, 'patch', split_axis=1, concat_axis=3, tiled=True)]
  transfers between devices with their start and end apart: 5 -> 18, of which waited for: 4 -> 12; matrix products, arithmetic and copies ran while one was open for 15% -> 13% of each run, Pallas kernels for 0% -> 0%
where the time goes in v1:
time: 264 us; the launch traced here: 263 us
  waiting for transfers between devices  146 us (55%)
  local copies, waits for them, and re-layouts  44.8 us (17%)
  starting transfers between devices  31.1 us (12%)
  between operations  14.7 us (6%)
  matrix products  10.6 us (4%)
  blocking collectives  8.05 us (3%)
  other arithmetic  7.68 us (3%)
    ppermute x14, waiting for transfers between devices, ring_gather(): x = lax.ppermute(x, axis, [(d, (d + 1) % ways) for d in range(ways)])  72.6 us
    all_gather x2, waiting for transfers between devices, fetch_weights(): lax.all_gather(qkv_rows, 'patch', axis=0, tiled=True)  66.3 us
    ppermute x14, starting transfers between devices, ring_gather(): x = lax.ppermute(x, axis, [(d, (d + 1) % ways) for d in range(ways)])  22.8 us
    dynamic_update_slice x13, local copies, waits for them, and re-layouts, ring_gather(): lax.dynamic_update_slice_in_dim(full, x, (here - far) % ways * step, axis...  9.68 us
    dot_general x2, matrix products, per_device(): joint = jnp.dot(mixed, qkv_full, preferred_element_type=jnp.float32)  7.92 us
    all_to_all x1, waiting for transfers between devices, spatial(): lax.all_to_all(attended, 'patch', split_axis=2, concat_axis=0, tiled=True)  7.27 us
    dot_general x1, local copies, waits for them, and re-layouts, per_device(): joint = jnp.dot(mixed, qkv_full, preferred_element_type=jnp.float32)  6.46 us
  transfers between devices with their start and end apart: 18, of which 12 were waited for; matrix products, arithmetic and copies ran while one was open for 13% of the time, Pallas kernels for 0%

profile of v1, /device:TPU:0, one launch (start us, length us, event | category | flops | bytes accessed | tf_op | source)
XLA Modules:
  0.0 263.2 jit_solution(6337880620391389853)
XLA Ops:
  6.5 2.3 fusion.34
  9.8 2.9 %collective-permute-start.7 = (bf16[576,144]{0,1:T(8,128)(2,1)}, bf16[576,144]{0,1:T(8,128)(2,1)}, u32[]{:S(2)}, u32[]{:S(2)}) collective-permute-start(bf16[576,144]{0,1:T(8,128)(2,1)} %get-tuple-element.27), channel_id=1, source_target_pairs={{0,2},{2,4},{4,6},{6,8},{8,10},{10,12},{12,14},{14,0},{1,3},{3,5},... | collective-permute-start | bytes 497672 | tf_op jit(solution)/shard_map/ppermute | solution.py:13
  12.7 1.5 collective-permute-start
  16.0 1.0 copy-done
  17.0 1.0 add_convert_fusion.1
  18.3 1.0 reshape.226
  19.2 1.1 copy.87
  22.2 2.5 collective-permute-done
  24.8 1.6 constant_dynamic-update-slice_fusion.6
  26.4 66.3 %all-gather.5.cloned.1.call-done = bf16[1,1152,1728]{2,1,0:T(8,128)(2,1)} async-done(((bf16[1,144,1728]{2,1,0:T(8,128)(2,1)}), bf16[1,1152,1728]{2,1,0:T(8,128)(2,1)}) %all-gather.5.cloned.1.call-update) | async-done | bytes 3981328 | tf_op jit(solution)/shard_map/all_gather | solution.py:42
  92.7 6.5 %copy.88 = bf16[1728,1152]{1,0:T(8,128)(2,1)} copy(bf16[1728,1152]{0,1:T(8,128)(2,1)} %bitcast.117) | data formatting | bytes 7962624 | tf_op jit(solution)/shard_map/dot_general | solution.py:122
  99.1 3.7 %fusion.13 = f32[160,3,8,72]{0,3,2,1:T(8,128)S(1)} fusion(bf16[3,8,72,1152]{3,2,1,0:T(8,128)(2,1)} %bitcast.118, bf16[160,1152,1,1]{1,0,2,3:T(8,128)(2,1)S(1)} %reshape.229), kind=kOutput, calls=%fused_computation.36 | convolution fusion | flops 637009920 | bytes 5455872 | tf_op jit(solution)/shard_map/dot_general | solution.py:122
  102.9 1.2 copy-done.8
  105.1 1.4 multiply_reduce_fusion.5
  108.4 1.2 multiply_convert_fusion.2
  110.3 1.1 copy.95
  111.4 3.6 %all-to-all-start = ((bf16[3,8,16,10,72]{4,2,3,0,1:T(8,128)(2,1)}), bf16[3,8,16,10,72]{4,2,3,0,1:T(8,128)(2,1)S(1)}, u32[]{:S(2)}, u32[]{:S(2)}) async-start(bf16[3,8,16,10,72]{4,2,3,0,1:T(8,128)(2,1)} %copy.95), calls=%async_computation | async-start | bytes 1966080 | tf_op jit(solution)/shard_map/all_to_all | solution.py:71
  115.0 1.0 constant_dynamic-update-slice_fusion.14
  115.9 2.0 collective-permute-start.9
  117.9 1.5 collective-permute-start.2
  119.4 1.6 constant_dynamic-update-slice_fusion.5
  121.9 27.6 %collective-permute-done.9 = bf16[576,144]{0,1:T(8,128)(2,1)S(1)} collective-permute-done((bf16[576,144]{0,1:T(8,128)(2,1)}, bf16[576,144]{0,1:T(8,128)(2,1)S(1)}, u32[]{:S(2)}, u32[]{:S(2)}) %collective-permute-start.9) | collective-permute-done | bytes 165920 | tf_op jit(solution)/shard_map/ppermute | solution.py:13
  149.5 7.9 %collective-permute-done.2 = bf16[576,144]{0,1:T(8,128)(2,1)S(1)} collective-permute-done((bf16[576,144]{0,1:T(8,128)(2,1)}, bf16[576,144]{0,1:T(8,128)(2,1)S(1)}, u32[]{:S(2)}, u32[]{:S(2)}) %collective-permute-start.2) | collective-permute-done | bytes 165920 | tf_op jit(solution)/shard_map/ppermute | solution.py:13
  158.1 7.2 %collective-permute-done.10 = bf16[576,144]{0,1:T(8,128)(2,1)S(1)} collective-permute-done((bf16[576,144]{0,1:T(8,128)(2,1)S(1)}, bf16[576,144]{0,1:T(8,128)(2,1)S(1)}, u32[]{:S(2)}, u32[]{:S(2)}) %collective-permute-start.10) | collective-permute-done | bytes 165920 | tf_op jit(solution)/shard_map/ppermute | solution.py:13
  165.5 7.7 %collective-permute-done.3 = bf16[576,144]{0,1:T(8,128)(2,1)S(1)} collective-permute-done((bf16[576,144]{0,1:T(8,128)(2,1)S(1)}, bf16[576,144]{0,1:T(8,128)(2,1)S(1)}, u32[]{:S(2)}, u32[]{:S(2)}) %collective-permute-start.3) | collective-permute-done | bytes 165920 | tf_op jit(solution)/shard_map/ppermute | solution.py:13
  173.2 2.9 %collective-permute-start.4 = (bf16[576,144]{0,1:T(8,128)(2,1)S(1)}, bf16[576,144]{0,1:T(8,128)(2,1)S(1)}, u32[]{:S(2)}, u32[]{:S(2)}) collective-permute-start(bf16[576,144]{0,1:T(8,128)(2,1)S(1)} %collective-permute-done.3), channel_id=1, source_target_pairs={{0,2},{2,4},{4,6},{6,8},{8,10},{10,12},{12,14},{14,0},{1,3},{3,5},... | collective-permute-start | bytes 497672 | tf_op jit(solution)/shard_map/ppermute | solution.py:13
  176.9 4.3 %collective-permute-done.11 = bf16[576,144]{0,1:T(8,128)(2,1)S(1)} collective-permute-done((bf16[576,144]{0,1:T(8,128)(2,1)S(1)}, bf16[576,144]{0,1:T(8,128)(2,1)S(1)}, u32[]{:S(2)}, u32[]{:S(2)}) %collective-permute-start.11) | collective-permute-done | bytes 165920 | tf_op jit(solution)/shard_map/ppermute | solution.py:13
  181.2 2.9 %collective-permute-start.12 = (bf16[576,144]{0,1:T(8,128)(2,1)S(1)}, bf16[576,144]{0,1:T(8,128)(2,1)S(1)}, u32[]{:S(2)}, u32[]{:S(2)}) collective-permute-start(bf16[576,144]{0,1:T(8,128)(2,1)S(1)} %collective-permute-done.11), channel_id=1, source_target_pairs={{0,2},{2,4},{4,6},{6,8},{8,10},{10,12},{12,14},{14,0},{1,3},{3,5},... | collective-permute-start | bytes 497672 | tf_op jit(solution)/shard_map/ppermute | solution.py:13
  184.1 4.9 %collective-permute-done.4 = bf16[576,144]{0,1:T(8,128)(2,1)S(1)} collective-permute-done((bf16[576,144]{0,1:T(8,128)(2,1)S(1)}, bf16[576,144]{0,1:T(8,128)(2,1)S(1)}, u32[]{:S(2)}, u32[]{:S(2)}) %collective-permute-start.4) | collective-permute-done | bytes 165920 | tf_op jit(solution)/shard_map/ppermute | solution.py:13
  189.0 2.8 %collective-permute-start.5 = (bf16[576,144]{0,1:T(8,128)(2,1)S(1)}, bf16[576,144]{0,1:T(8,128)(2,1)S(1)}, u32[]{:S(2)}, u32[]{:S(2)}) collective-permute-start(bf16[576,144]{0,1:T(8,128)(2,1)S(1)} %collective-permute-done.4), channel_id=1, source_target_pairs={{0,2},{2,4},{4,6},{6,8},{8,10},{10,12},{12,14},{14,0},{1,3},{3,5},... | collective-permute-start | bytes 497672 | tf_op jit(solution)/shard_map/ppermute | solution.py:13
  192.5 4.4 %collective-permute-done.12 = bf16[576,144]{0,1:T(8,128)(2,1)S(1)} collective-permute-done((bf16[576,144]{0,1:T(8,128)(2,1)S(1)}, bf16[576,144]{0,1:T(8,128)(2,1)S(1)}, u32[]{:S(2)}, u32[]{:S(2)}) %collective-permute-start.12) | collective-permute-done | bytes 165920 | tf_op jit(solution)/shard_map/ppermute | solution.py:13
  196.9 2.8 %collective-permute-start.13 = (bf16[576,144]{0,1:T(8,128)(2,1)S(1)}, bf16[576,144]{0,1:T(8,128)(2,1)S(1)}, u32[]{:S(2)}, u32[]{:S(2)}) collective-permute-start(bf16[576,144]{0,1:T(8,128)(2,1)S(1)} %collective-permute-done.12), channel_id=1, source_target_pairs={{0,2},{2,4},{4,6},{6,8},{8,10},{10,12},{12,14},{14,0},{1,3},{3,5},... | collective-permute-start | bytes 497672 | tf_op jit(solution)/shard_map/ppermute | solution.py:13
  199.7 5.1 %collective-permute-done.5 = bf16[576,144]{0,1:T(8,128)(2,1)S(1)} collective-permute-done((bf16[576,144]{0,1:T(8,128)(2,1)S(1)}, bf16[576,144]{0,1:T(8,128)(2,1)S(1)}, u32[]{:S(2)}, u32[]{:S(2)}) %collective-permute-start.5) | collective-permute-done | bytes 165920 | tf_op jit(solution)/shard_map/ppermute | solution.py:13
  204.8 2.7 %collective-permute-start.6 = (bf16[576,144]{0,1:T(8,128)(2,1)S(1)}, bf16[576,144]{0,1:T(8,128)(2,1)}, u32[]{:S(2)}, u32[]{:S(2)}) collective-permute-start(bf16[576,144]{0,1:T(8,128)(2,1)S(1)} %collective-permute-done.5), channel_id=1, source_target_pairs={{0,2},{2,4},{4,6},{6,8},{8,10},{10,12},{12,14},{14,0},{1,3},{3,5},... | collective-permute-start | bytes 497672 | tf_op jit(solution)/shard_map/ppermute | solution.py:13
  208.4 1.0 copy.100
  209.4 4.6 %all-to-all-start.1 = ((bf16[1,16,80,72]{3,1,0,2:T(8,128)(2,1)}), bf16[1,16,80,72]{3,1,0,2:T(8,128)(2,1)S(1)}, u32[]{:S(2)}, u32[]{:S(2)}) async-start(bf16[1,16,80,72]{3,1,0,2:T(8,128)(2,1)} %copy.100), calls=%async_computation.1 | async-start | bytes 655360 | tf_op jit(solution)/shard_map/all_to_all | solution.py:73
  214.8 1.7 constant_dynamic-update-slice_fusion
  216.5 7.3 %all-to-all-done.1 = bf16[1,16,80,72]{3,1,0,2:T(8,128)(2,1)S(1)} async-done(((bf16[1,16,80,72]{3,1,0,2:T(8,128)(2,1)}), bf16[1,16,80,72]{3,1,0,2:T(8,128)(2,1)S(1)}, u32[]{:S(2)}, u32[]{:S(2)}) %all-to-all-start.1) | async-done | bytes 184352 | tf_op jit(solution)/shard_map/all_to_all | solution.py:73
  225.1 4.2 %fusion = f32[160,1728]{1,0:T(8,128)} fusion(bf16[1,1152,1728]{2,1,0:T(8,128)(2,1)} %all-gather.7.cloned.1.call-done, f32[160,1152]{1,0:T(8,128)S(1)} %get-tuple-element.42, f32[1152]{0:T(1024)S(1)} %get-tuple-element.10, f32[1152]{0:T(1024)S(1)} %get-tuple-element.11, f32[160]{0:T(256)S(1)} %add_rsqrt_fusion.5, f32[160]{0:T(256)S(1)} %broadcast_multiply_fusion.1), kind=kOutput, calls=%fused_computation | convolution fusion | flops 637931520 | bytes 5835008 | tf_op jit(solution)/shard_map/dot_general | solution.py:122
  229.2 2.2 reshape.219
  231.4 1.1 multiply_reduce_fusion.2
  233.3 1.4 squeeze.62
  235.9 1.1 mul.307
  237.0 1.4 mul.308
  238.4 2.1 convert_element_type.113
  242.4 1.3 concatenate.8
  243.9 4.2 %all_to_all.63 = bf16[2,8,10,1728]{3,1,0,2:T(8,128)(2,1)S(1)} all-to-all(bf16[2,8,10,1728]{3,1,0,2:T(8,128)(2,1)S(1)} %copy.108), channel_id=1, replica_groups=mesh['grp'=2,'patch'=8,'frame'=2] {'frame'}, dimensions={2} | all-to-all | bytes 1105920 | tf_op jit(solution)/shard_map/all_to_all | solution.py:104
  250.8 3.9 %all_to_all.64 = bf16[2,16,5,576]{3,0,2,1:T(2,128)(2,1)S(1)} all-to-all(bf16[2,16,5,576]{3,0,2,1:T(2,128)(2,1)S(1)} %reshape.231), channel_id=1, replica_groups=mesh['grp'=2,'patch'=8,'frame'=2] {'frame'}, dimensions={1} | all-to-all | bytes 368640 | tf_op jit(solution)/shard_map/all_to_all | solution.py:108
  (119 shorter events, 21.8 us)
Async XLA Ops:
  6.5 2.4 copy-start.4
  6.5 8.5 %copy-start.9 = (f32[2,3,1152]{2,0,1:T(2,128)S(1)}, f32[2,3,1152]{2,0,1:T(2,128)}, u32[]{:S(2)}) copy-start(f32[2,3,1152]{2,0,1:T(2,128)} %param.13) | copy-start | bytes 82948
  6.5 8.5 %copy-start.10 = (f32[2,3,1152]{2,0,1:T(2,128)S(1)}, f32[2,3,1152]{2,0,1:T(2,128)}, u32[]{:S(2)}) copy-start(f32[2,3,1152]{2,0,1:T(2,128)} %param.12) | copy-start | bytes 82948
  6.5 86.1 %all-gather.5.cloned.1.call-start = ((), (), s32[]{:S(2)}) async-start(), calls=%async_computation.4 | async-start | bytes 4644864 | tf_op jit(solution)/shard_map/all_gather | solution.py:42
  8.9 6.4 %copy-start.2 = (bf16[2,8,10,1152]{3,1,2,0:T(8,128)(2,1)S(1)}, bf16[2,8,10,1152]{3,1,2,0:T(8,128)(2,1)}, u32[]{:S(2)}) copy-start(bf16[2,8,10,1152]{3,1,2,0:T(8,128)(2,1)} %param.7) | copy-start | bytes 1105924
  8.9 216.1 %all-gather.7.cloned.1.call-start = ((), (), s32[]{:S(2)}) async-start(), calls=%async_computation.5 | async-start | bytes 4644864 | tf_op jit(solution)/shard_map/all_gather | solution.py:42
  9.8 11.8 %collective-permute-start.7 = (bf16[576,144]{0,1:T(8,128)(2,1)}, bf16[576,144]{0,1:T(8,128)(2,1)}, u32[]{:S(2)}, u32[]{:S(2)}) collective-permute-start(bf16[576,144]{0,1:T(8,128)(2,1)} %get-tuple-element.27), channel_id=1, source_target_pairs={{0,2},{2,4},{4,6},{6,8},{8,10},{10,12},{12,14},{14,0},{1,3},{3,5},... | collective-permute-start | bytes 497672 | tf_op jit(solution)/shard_map/ppermute | solution.py:13
  12.7 12.0 %collective-permute-start = (bf16[576,144]{0,1:T(8,128)(2,1)}, bf16[576,144]{0,1:T(8,128)(2,1)}, u32[]{:S(2)}, u32[]{:S(2)}) collective-permute-start(bf16[576,144]{0,1:T(8,128)(2,1)} %get-tuple-element.28), channel_id=1, source_target_pairs={{0,2},{2,4},{4,6},{6,8},{8,10},{10,12},{12,14},{14,0},{1,3},{3,5},... | collective-permute-start | bytes 497672 | tf_op jit(solution)/shard_map/ppermute | solution.py:13
  15.8 2.3 copy-start.11
  15.8 1.2 copy-start
  21.5 94.4 %collective-permute-start.8 = (bf16[576,144]{0,1:T(8,128)(2,1)}, bf16[576,144]{0,1:T(8,128)(2,1)}, u32[]{:S(2)}, u32[]{:S(2)}) collective-permute-start(bf16[576,144]{0,1:T(8,128)(2,1)} %collective-permute-done.7), channel_id=1, source_target_pairs={{0,2},{2,4},{4,6},{6,8},{8,10},{10,12},{12,14},{14,0},{1,3},{3,5},... | collective-permute-start | bytes 497672 | tf_op jit(solution)/shard_map/ppermute | solution.py:13
  24.8 93.1 %collective-permute-start.1 = (bf16[576,144]{0,1:T(8,128)(2,1)}, bf16[576,144]{0,1:T(8,128)(2,1)}, u32[]{:S(2)}, u32[]{:S(2)}) collective-permute-start(bf16[576,144]{0,1:T(8,128)(2,1)} %collective-permute-done), channel_id=1, source_target_pairs={{0,2},{2,4},{4,6},{6,8},{8,10},{10,12},{12,14},{14,0},{1,3},{3,5},... | collective-permute-start | bytes 497672 | tf_op jit(solution)/shard_map/ppermute | solution.py:13
  102.9 1.2 copy-start.8
  108.1 1.7 copy-start.5
  111.4 96.1 %all-to-all-start = ((bf16[3,8,16,10,72]{4,2,3,0,1:T(8,128)(2,1)}), bf16[3,8,16,10,72]{4,2,3,0,1:T(8,128)(2,1)S(1)}, u32[]{:S(2)}, u32[]{:S(2)}) async-start(bf16[3,8,16,10,72]{4,2,3,0,1:T(8,128)(2,1)} %copy.95), calls=%async_computation | async-start | bytes 1966080 | tf_op jit(solution)/shard_map/all_to_all | solution.py:71
  115.9 33.6 %collective-permute-start.9 = (bf16[576,144]{0,1:T(8,128)(2,1)}, bf16[576,144]{0,1:T(8,128)(2,1)S(1)}, u32[]{:S(2)}, u32[]{:S(2)}) collective-permute-start(bf16[576,144]{0,1:T(8,128)(2,1)} %collective-permute-done.8), channel_id=1, source_target_pairs={{0,2},{2,4},{4,6},{6,8},{8,10},{10,12},{12,14},{14,0},{1,3},{3,5},... | collective-permute-start | bytes 497672 | tf_op jit(solution)/shard_map/ppermute | solution.py:13
  117.9 39.5 %collective-permute-start.2 = (bf16[576,144]{0,1:T(8,128)(2,1)}, bf16[576,144]{0,1:T(8,128)(2,1)S(1)}, u32[]{:S(2)}, u32[]{:S(2)}) collective-permute-start(bf16[576,144]{0,1:T(8,128)(2,1)} %collective-permute-done.1), channel_id=1, source_target_pairs={{0,2},{2,4},{4,6},{6,8},{8,10},{10,12},{12,14},{14,0},{1,3},{3,5},... | collective-permute-start | bytes 497672 | tf_op jit(solution)/shard_map/ppermute | solution.py:13
  149.5 15.9 %collective-permute-start.10 = (bf16[576,144]{0,1:T(8,128)(2,1)S(1)}, bf16[576,144]{0,1:T(8,128)(2,1)S(1)}, u32[]{:S(2)}, u32[]{:S(2)}) collective-permute-start(bf16[576,144]{0,1:T(8,128)(2,1)S(1)} %collective-permute-done.9), channel_id=1, source_target_pairs={{0,2},{2,4},{4,6},{6,8},{8,10},{10,12},{12,14},{14,0},{1,3},{3,5},... | collective-permute-start | bytes 497672 | tf_op jit(solution)/shard_map/ppermute | solution.py:13
  157.4 15.8 %collective-permute-start.3 = (bf16[576,144]{0,1:T(8,128)(2,1)S(1)}, bf16[576,144]{0,1:T(8,128)(2,1)S(1)}, u32[]{:S(2)}, u32[]{:S(2)}) collective-permute-start(bf16[576,144]{0,1:T(8,128)(2,1)S(1)} %collective-permute-done.2), channel_id=1, source_target_pairs={{0,2},{2,4},{4,6},{6,8},{8,10},{10,12},{12,14},{14,0},{1,3},{3,5},... | collective-permute-start | bytes 497672 | tf_op jit(solution)/shard_map/ppermute | solution.py:13
  165.4 15.8 %collective-permute-start.11 = (bf16[576,144]{0,1:T(8,128)(2,1)S(1)}, bf16[576,144]{0,1:T(8,128)(2,1)S(1)}, u32[]{:S(2)}, u32[]{:S(2)}) collective-permute-start(bf16[576,144]{0,1:T(8,128)(2,1)S(1)} %collective-permute-done.10), channel_id=1, source_target_pairs={{0,2},{2,4},{4,6},{6,8},{8,10},{10,12},{12,14},{14,0},{1,3},{3,5},... | collective-permute-start | bytes 497672 | tf_op jit(solution)/shard_map/ppermute | solution.py:13
  173.2 15.8 %collective-permute-start.4 = (bf16[576,144]{0,1:T(8,128)(2,1)S(1)}, bf16[576,144]{0,1:T(8,128)(2,1)S(1)}, u32[]{:S(2)}, u32[]{:S(2)}) collective-permute-start(bf16[576,144]{0,1:T(8,128)(2,1)S(1)} %collective-permute-done.3), channel_id=1, source_target_pairs={{0,2},{2,4},{4,6},{6,8},{8,10},{10,12},{12,14},{14,0},{1,3},{3,5},... | collective-permute-start | bytes 497672 | tf_op jit(solution)/shard_map/ppermute | solution.py:13
  181.2 15.7 %collective-permute-start.12 = (bf16[576,144]{0,1:T(8,128)(2,1)S(1)}, bf16[576,144]{0,1:T(8,128)(2,1)S(1)}, u32[]{:S(2)}, u32[]{:S(2)}) collective-permute-start(bf16[576,144]{0,1:T(8,128)(2,1)S(1)} %collective-permute-done.11), channel_id=1, source_target_pairs={{0,2},{2,4},{4,6},{6,8},{8,10},{10,12},{12,14},{14,0},{1,3},{3,5},... | collective-permute-start | bytes 497672 | tf_op jit(solution)/shard_map/ppermute | solution.py:13
  189.0 15.8 %collective-permute-start.5 = (bf16[576,144]{0,1:T(8,128)(2,1)S(1)}, bf16[576,144]{0,1:T(8,128)(2,1)S(1)}, u32[]{:S(2)}, u32[]{:S(2)}) collective-permute-start(bf16[576,144]{0,1:T(8,128)(2,1)S(1)} %collective-permute-done.4), channel_id=1, source_target_pairs={{0,2},{2,4},{4,6},{6,8},{8,10},{10,12},{12,14},{14,0},{1,3},{3,5},... | collective-permute-start | bytes 497672 | tf_op jit(solution)/shard_map/ppermute | solution.py:13
  196.9 17.8 %collective-permute-start.13 = (bf16[576,144]{0,1:T(8,128)(2,1)S(1)}, bf16[576,144]{0,1:T(8,128)(2,1)S(1)}, u32[]{:S(2)}, u32[]{:S(2)}) collective-permute-start(bf16[576,144]{0,1:T(8,128)(2,1)S(1)} %collective-permute-done.12), channel_id=1, source_target_pairs={{0,2},{2,4},{4,6},{6,8},{8,10},{10,12},{12,14},{14,0},{1,3},{3,5},... | collective-permute-start | bytes 497672 | tf_op jit(solution)/shard_map/ppermute | solution.py:13
  204.8 9.9 %collective-permute-start.6 = (bf16[576,144]{0,1:T(8,128)(2,1)S(1)}, bf16[576,144]{0,1:T(8,128)(2,1)}, u32[]{:S(2)}, u32[]{:S(2)}) collective-permute-start(bf16[576,144]{0,1:T(8,128)(2,1)S(1)} %collective-permute-done.5), channel_id=1, source_target_pairs={{0,2},{2,4},{4,6},{6,8},{8,10},{10,12},{12,14},{14,0},{1,3},{3,5},... | collective-permute-start | bytes 497672 | tf_op jit(solution)/shard_map/ppermute | solution.py:13
  209.4 14.3 %all-to-all-start.1 = ((bf16[1,16,80,72]{3,1,0,2:T(8,128)(2,1)}), bf16[1,16,80,72]{3,1,0,2:T(8,128)(2,1)S(1)}, u32[]{:S(2)}, u32[]{:S(2)}) async-start(bf16[1,16,80,72]{3,1,0,2:T(8,128)(2,1)} %copy.100), calls=%async_computation.1 | async-start | bytes 655360 | tf_op jit(solution)/shard_map/all_to_all | solution.py:73
  214.7 9.4 %copy-start.3 = (f32[160,1152]{1,0:T(8,128)S(1)}, f32[160,1152]{1,0:T(8,128)}, u32[]{:S(2)}) copy-start(f32[160,1152]{1,0:T(8,128)} %reshape.226) | copy-start | bytes 2211844
  241.3 1.0 copy-start.6
  241.3 1.2 copy-start.7
  250.0 4.8 %copy-start.1 = (bf16[576,1152]{0,1:T(8,128)(2,1)S(1)}, bf16[576,1152]{0,1:T(8,128)(2,1)}, u32[]{:S(2)}) copy-start(bf16[576,1152]{0,1:T(8,128)(2,1)} %get-tuple-element.49) | copy-start | bytes 3981316
Sparse Core Ops, SparseCore 0:
  9.6 83.0 all-gather.4
  94.9 95.0 all-gather.6
